TPU v7x, 256 devices: a whole 4x4x8 slice. The times are simulated.
256 devices in a mesh: seq: 32 (over z, x), head: 8 (over y, core).
Axes of the slice: x: 4, y: 4, z: 8, core: 2. Of those that a mesh axis runs over, the one named last changes fastest.
Arguments:
- queries: bfloat16 [16384, 1024], P(('seq', 'head')), may hold values from -24 to 24
- keys: bfloat16 [16384, 1024], P(('seq', 'head')), may hold values from -6 to 6
- values: bfloat16 [16384, 1024], P(('seq', 'head')), may hold values from -6 to 6
- out_grad: bfloat16 [16384, 1024], P(('seq', 'head')), may hold values from -6 to 6
- key_blocks: int32 [128, 8], replicated, may hold values from 0 to 127, as said below
- counts: int32 [128], replicated, may hold values from 2 to 8, as said below
Outputs:
- attention: bfloat16 [16384, 1024], P('seq', 'head')
- query_grad: bfloat16 [16384, 1024], P('seq', 'head')
- key_grad: bfloat16 [16384, 1024], P('seq', 'head')
- value_grad: bfloat16 [16384, 1024], P('seq', 'head')
Inputs may be any that keep to these rules, and one draw needn't show every extreme that they name: `counts`: some query block uses all 8 listed blocks. `key_blocks`: row a lists 8 different blocks, the first being block a itself and the second block (a - 1) modulo 128; only the first counts[a] of them are used.
All inputs are finite; a program needn't handle non-finite values.
Results may differ from a plain program's by a relative error of at most 0.015.
Values may be sent and summed in bfloat16 or wider, within the bound.
A program may use at most 64 MiB of HBM per device.

v0:
```python
import math

import jax
import jax.numpy as jnp
from jax import lax
from jax.sharding import PartitionSpec as P

HEADS = 8
BLK = 128


neg_fill = -1e30
tile_limit = 512


def block_table(key_blocks, counts):
    block_count = key_blocks.shape[0]
    slot_ids = jnp.arange(key_blocks.shape[1])
    live_slot = slot_ids[None, :] < counts[:, None]
    matches = (key_blocks[:, :, None] == jnp.arange(block_count)[None, None, :]) & live_slot[
        :, :, None
    ]
    return jnp.any(matches, axis=1).astype(jnp.float32)


def one_hot_rows(first_row, row_total, block_count):
    block_ids = (first_row + jnp.arange(row_total)) // BLK
    return (block_ids[:, None] == jnp.arange(block_count)[None, :]).astype(jnp.float32)


def on_device(queries, keys, values, out_grad, key_blocks, counts):
    heads_here = HEADS // lax.axis_size("head")
    q_rows, k_rows, v_rows, g_rows = (
        lax.all_to_all(queries, "head", split_axis=1, concat_axis=0, tiled=True),
        lax.all_to_all(keys, "head", split_axis=1, concat_axis=0, tiled=True),
        lax.all_to_all(values, "head", split_axis=1, concat_axis=0, tiled=True),
        lax.all_to_all(out_grad, "head", split_axis=1, concat_axis=0, tiled=True),
    )
    row_count = q_rows.shape[0]
    feat_width = q_rows.shape[1]
    head_dim = feat_width // heads_here
    score_scale = 1.0 / math.sqrt(head_dim)
    block_count = key_blocks.shape[0]
    slot_total = key_blocks.shape[1]
    local_blocks = row_count // BLK
    first_block = lax.axis_index("seq") * local_blocks
    listed = lax.dynamic_slice_in_dim(key_blocks, first_block, local_blocks, 0)
    used = lax.dynamic_slice_in_dim(counts, first_block, local_blocks, 0)
    slot_ids = jnp.arange(slot_total)
    live = jnp.repeat(slot_ids[None, :] < used[:, None], BLK, axis=1)
    live_mask = live[:, None, None, :]

    def listed_sets(k_whole, v_whole):
        k_blocks = k_whole.reshape(block_count, BLK, heads_here, head_dim)
        v_blocks = v_whole.reshape(block_count, BLK, heads_here, head_dim)
        key_set = jnp.take(k_blocks, listed, axis=0).reshape(
            local_blocks, slot_total * BLK, heads_here, head_dim
        )
        value_set = jnp.take(v_blocks, listed, axis=0).reshape(
            local_blocks, slot_total * BLK, heads_here, head_dim
        )
        return (key_set, value_set)

    q_blocks = q_rows.reshape(local_blocks, BLK, heads_here, head_dim)
    g_blocks = g_rows.reshape(local_blocks, BLK, heads_here, head_dim)

    def block_scores(key_set):
        scores = (
            jnp.einsum("bqhd,bkhd->bhqk", q_blocks, key_set, preferred_element_type=jnp.float32)
            * score_scale
        )
        return jnp.where(live_mask, scores, neg_fill)

    k_whole, v_whole = (
        lax.all_gather(k_rows, "seq", axis=0, tiled=True),
        lax.all_gather(v_rows, "seq", axis=0, tiled=True),
    )
    key_set, value_set = listed_sets(k_whole, v_whole)
    scores = block_scores(key_set)
    row_max = jnp.max(scores, axis=3)
    weights = jnp.where(live_mask, jnp.exp(scores - row_max[..., None]), 0.0)
    row_sum = jnp.sum(weights, axis=3)
    mixed = jnp.einsum(
        "bhqk,bkhd->bqhd",
        weights.astype(jnp.bfloat16),
        value_set,
        preferred_element_type=jnp.float32,
    )
    attention = (mixed / jnp.transpose(row_sum, (0, 2, 1))[..., None]).astype(jnp.bfloat16)
    block_total = row_max + jnp.log(row_sum)
    block_dot = jnp.sum(g_blocks.astype(jnp.float32) * attention.astype(jnp.float32), axis=3)
    dot_bhq = jnp.transpose(block_dot, (0, 2, 1))
    log_total = jnp.transpose(block_total, (0, 2, 1)).reshape(row_count, heads_here)
    grad_dot = block_dot.reshape(row_count, heads_here)
    k_second, v_second = (
        lax.all_gather(k_rows, "seq", axis=0, tiled=True),
        lax.all_gather(v_rows, "seq", axis=0, tiled=True),
    )
    key_again, value_again = listed_sets(k_second, v_second)
    scores_again = block_scores(key_again)
    probs = jnp.where(live_mask, jnp.exp(scores_again - block_total[..., None]), 0.0)
    dprob = jnp.einsum("bqhd,bkhd->bhqk", g_blocks, value_again, preferred_element_type=jnp.float32)
    dscore = (probs * (dprob - dot_bhq[..., None])).astype(jnp.bfloat16)
    query_acc = jnp.einsum("bhqk,bkhd->bqhd", dscore, key_again, preferred_element_type=jnp.float32)
    all_log_total, all_grad_dot = (
        lax.all_gather(log_total, "seq", axis=0, tiled=True),
        lax.all_gather(grad_dot, "seq", axis=0, tiled=True),
    )
    table = block_table(key_blocks, counts)
    local_hot = one_hot_rows(lax.axis_index("seq") * row_count, row_count, block_count)
    key_table = jnp.einsum("bc,kc->bk", table, local_hot)
    k_heads = k_rows.reshape(row_count, heads_here, head_dim)
    v_heads = v_rows.reshape(row_count, heads_here, head_dim)
    zero_heads = jnp.zeros((row_count, heads_here, head_dim), jnp.float32)
    q_piece = lax.all_gather(q_rows, "seq", axis=0, tiled=True)
    g_piece = lax.all_gather(g_rows, "seq", axis=0, tiled=True)
    piece_rows = q_piece.shape[0]
    tile_rows = math.gcd(piece_rows, tile_limit)

    def tile(tile_index, fold_state):
        offset = tile_index * tile_rows
        q_tile = lax.dynamic_slice_in_dim(q_piece, offset, tile_rows, 0).reshape(
            tile_rows, heads_here, head_dim
        )
        g_tile = lax.dynamic_slice_in_dim(g_piece, offset, tile_rows, 0).reshape(
            tile_rows, heads_here, head_dim
        )
        total_tile = lax.dynamic_slice_in_dim(all_log_total, offset, tile_rows, 0)
        dot_tile = lax.dynamic_slice_in_dim(all_grad_dot, offset, tile_rows, 0)
        query_hot = one_hot_rows(offset, tile_rows, block_count)
        allowed = jnp.einsum("qb,bk->qk", query_hot, key_table) > 0.5
        tile_scores = (
            jnp.einsum("qhd,khd->qhk", q_tile, k_heads, preferred_element_type=jnp.float32)
            * score_scale
        )
        tile_scores = jnp.where(allowed[:, None, :], tile_scores, neg_fill)
        tile_probs = jnp.where(
            allowed[:, None, :], jnp.exp(tile_scores - total_tile[:, :, None]), 0.0
        )
        value_acc = fold_state[1] + jnp.einsum(
            "qhk,qhd->khd",
            tile_probs.astype(jnp.bfloat16),
            g_tile,
            preferred_element_type=jnp.float32,
        )
        tile_dprob = jnp.einsum("qhd,khd->qhk", g_tile, v_heads, preferred_element_type=jnp.float32)
        tile_ds = (tile_probs * (tile_dprob - dot_tile[:, :, None])).astype(jnp.bfloat16)
        key_acc = fold_state[0] + jnp.einsum(
            "qhk,qhd->khd", tile_ds, q_tile, preferred_element_type=jnp.float32
        )
        return (key_acc, value_acc)

    key_acc, value_acc = lax.fori_loop(0, piece_rows // tile_rows, tile, (zero_heads, zero_heads))
    query_grad = (query_acc * score_scale).astype(jnp.bfloat16).reshape(row_count, feat_width)
    key_grad = (key_acc * score_scale).astype(jnp.bfloat16).reshape(row_count, feat_width)
    value_grad = value_acc.astype(jnp.bfloat16).reshape(row_count, feat_width)
    return (attention.reshape(row_count, feat_width), query_grad, key_grad, value_grad)


def solution(mesh):
    in_specs = (
        P(("seq", "head"), None),
        P(("seq", "head"), None),
        P(("seq", "head"), None),
        P(("seq", "head"), None),
        P(),
        P(),
    )
    out_specs = (P("seq", "head"), P("seq", "head"), P("seq", "head"), P("seq", "head"))
    return jax.shard_map(
        on_device, mesh=mesh, in_specs=in_specs, out_specs=out_specs, check_vma=False
    )
```

profile of v0, /device:TPU:8, one launch (start us, length us, event | category | flops | bytes accessed | tf_op | source)
XLA Modules:
  0.0 496.2 jit_solution(53246647357267488)
XLA Ops:
  8.1 9.9 %all_to_all.76 = bf16[64,8,128]{2,0,1:T(8,128)(2,1)} all-to-all(bf16[64,8,128]{2,0,1:T(8,128)(2,1)S(1)} %copy_bitcast_fusion.2), channel_id=1, replica_groups=mesh['seq'=32,'head'=8] {'head'}, dimensions={1} | all-to-all | bytes 262144 | tf_op jit(solution)/shard_map/all_to_all | solution.py:35
  19.0 9.2 %all_to_all.77 = bf16[64,8,128]{2,0,1:T(8,128)(2,1)} all-to-all(bf16[64,8,128]{2,0,1:T(8,128)(2,1)S(1)} %copy_bitcast_fusion.3), channel_id=1, replica_groups=mesh['seq'=32,'head'=8] {'head'}, dimensions={1} | all-to-all | bytes 262144 | tf_op jit(solution)/shard_map/all_to_all | solution.py:36
  29.1 9.2 %all_to_all.78 = bf16[64,8,128]{2,0,1:T(8,128)(2,1)} all-to-all(bf16[64,8,128]{2,0,1:T(8,128)(2,1)S(1)} %copy_bitcast_fusion.1), channel_id=1, replica_groups=mesh['seq'=32,'head'=8] {'head'}, dimensions={1} | all-to-all | bytes 262144 | tf_op jit(solution)/shard_map/all_to_all | solution.py:34
  39.3 9.2 %all_to_all.79 = bf16[64,8,128]{2,0,1:T(8,128)(2,1)} all-to-all(bf16[64,8,128]{2,0,1:T(8,128)(2,1)S(1)} %copy_bitcast_fusion), channel_id=1, replica_groups=mesh['seq'=32,'head'=8] {'head'}, dimensions={1} | all-to-all | bytes 262144 | tf_op jit(solution)/shard_map/all_to_all | solution.py:37
  50.0 51.3 %all-gather.7.cloned.1.call-done = bf16[16384,128]{1,0:T(8,128)(2,1)} async-done(((bf16[512,128]{1,0:T(8,128)(2,1)}), bf16[16384,128]{1,0:T(8,128)(2,1)}) %all-gather.7.cloned.1.call-update) | async-done | bytes 4194320 | tf_op jit(solution)/shard_map/all_gather | solution.py:75
  101.3 2.9 gather_fusion.1
  104.3 78.2 %all-gather.5.cloned.1.call-done = bf16[16384,128]{1,0:T(8,128)(2,1)} async-done(((bf16[512,128]{1,0:T(8,128)(2,1)}), bf16[16384,128]{1,0:T(8,128)(2,1)}) %all-gather.5.cloned.1.call-update) | async-done | bytes 4194320 | tf_op jit(solution)/shard_map/all_gather | solution.py:76
  182.5 2.9 gather_fusion
  188.5 47.6 %all_gather.23 = f32[16384,1]{0,1:T(1,128)S(1)} all-gather(f32[512,1]{0,1:T(1,128)S(1)} %bitcast.245), channel_id=1, replica_groups=mesh['seq'=32,'head'=8] {'seq'}, dimensions={0}, use_global_device_ids=true | all-gather | bytes 67584 | tf_op jit(solution)/shard_map/all_gather | solution.py:106
  236.1 2.7 fusion.54
  238.8 47.4 %all_gather.25 = f32[16384,1]{0,1:T(1,128)S(1)} all-gather(f32[512,1]{0,1:T(1,128)S(1)} %bitcast.246), channel_id=1, replica_groups=mesh['seq'=32,'head'=8] {'seq'}, dimensions={0}, use_global_device_ids=true | all-gather | bytes 67584 | tf_op jit(solution)/shard_map/all_gather | solution.py:107
  286.1 3.5 fusion.41
  289.6 55.2 %all-gather.11.cloned.1.call-done = bf16[16384,128]{1,0:T(8,128)(2,1)} async-done(((bf16[512,128]{1,0:T(8,128)(2,1)}), bf16[16384,128]{1,0:T(8,128)(2,1)}) %all-gather.11.cloned.1.call-update) | async-done | bytes 4194320 | tf_op jit(solution)/shard_map/all_gather | solution.py:116
  344.8 143.3 %while.18 = (s32[]{:T(128)}, f32[512,1,128]{0,2,1:T(8,128)S(1)}, f32[512,1,128]{0,2,1:T(8,128)S(1)}, bf16[16384,128]{1,0:T(8,128)(2,1)}, bf16[128,512]{1,0:T(8,1...) while((s32[]{:T(128)}, f32[512,1,128]{0,2,1:T(8,128)S(1)}, ...), condition=%wide.region_5.7_spmd.clone, body=%wide.region_4.6_spmd.clone.sunk | while | flops 338239488 | bytes 5654229 | solution.py:153
  345.2 1.4 fusion.96
  346.6 1.5 fusion.97
  349.7 1.4 fusion.96
  351.1 1.5 fusion.97
  354.2 1.4 fusion.96
  355.5 1.5 fusion.97
  358.6 1.4 fusion.96
  360.0 1.5 fusion.97
  363.1 1.4 fusion.96
  364.5 1.5 fusion.97
  367.6 1.4 fusion.96
  369.0 1.5 fusion.97
  372.1 1.4 fusion.96
  373.5 1.5 fusion.97
  376.6 1.4 fusion.96
  377.9 1.5 fusion.97
  381.0 1.4 fusion.96
  382.4 1.5 fusion.97
  385.5 1.4 fusion.96
  386.9 1.5 fusion.97
  390.0 1.4 fusion.96
  391.4 1.5 fusion.97
  395.8 1.5 fusion.97
  400.3 1.5 fusion.97
  403.4 1.4 fusion.96
  404.8 1.5 fusion.97
  409.3 1.5 fusion.97
  413.7 1.5 fusion.97
  416.8 1.4 fusion.96
  418.2 1.5 fusion.97
  422.7 1.5 fusion.97
  427.2 1.5 fusion.97
  430.3 1.4 fusion.96
  431.7 1.5 fusion.97
  436.1 1.5 fusion.97
  440.6 1.5 fusion.97
  443.7 1.4 fusion.96
  445.1 1.5 fusion.97
  449.6 1.5 fusion.97
  454.0 1.5 fusion.97
  457.1 1.4 fusion.96
  458.5 1.5 fusion.97
  463.0 1.5 fusion.97
  467.5 1.5 fusion.97
  470.6 1.4 fusion.96
  472.0 1.5 fusion.97
  476.4 1.5 fusion.97
  480.9 1.5 fusion.97
  484.0 1.4 fusion.96
  485.4 1.5 fusion.97
  (196 shorter events, 78.6 us)
Async XLA Ops:
  7.2 0.9 copy-start
  7.2 41.3 %copy-start.7 = (s32[128,8]{0,1:T(8,128)S(1)}, s32[128,8]{0,1:T(8,128)}, u32[]{:S(2)}) copy-start(s32[128,8]{0,1:T(8,128)} %param.14) | copy-start | bytes 12292
  7.2 41.8 %copy-start.8 = (s32[128]{0:T(128)S(1)}, s32[128]{0:T(128)}, u32[]{:S(2)}) copy-start(s32[128]{0:T(128)} %param.15) | copy-start | bytes 1540
  7.2 94.1 %all-gather.7.cloned.1.call-start = ((), (), s32[]{:S(2)}) async-start(), calls=%async_computation.5 | async-start | bytes 4325376 | tf_op jit(solution)/shard_map/all_gather | solution.py:75
  18.0 164.5 %all-gather.5.cloned.1.call-start = ((), (), s32[]{:S(2)}) async-start(), calls=%async_computation.4 | async-start | bytes 4325376 | tf_op jit(solution)/shard_map/all_gather | solution.py:76
  28.2 261.5 %all-gather.9.cloned.1.call-start = ((), (), s32[]{:S(2)}) async-start(), calls=%async_computation.6 | async-start | bytes 4325376 | tf_op jit(solution)/shard_map/all_gather | solution.py:115
  38.3 306.5 %all-gather.11.cloned.1.call-start = ((), (), s32[]{:S(2)}) async-start(), calls=%async_computation.7 | async-start | bytes 4325376 | tf_op jit(solution)/shard_map/all_gather | solution.py:116
  185.4 0.9 copy-start.5
  185.7 2.7 copy-start.2
  185.7 50.3 %copy-start.3 = (bf16[4,8,128,1,128]{4,2,1,0,3:T(8,128)(2,1)}, bf16[4,8,128,1,128]{4,2,1,0,3:T(8,128)(2,1)S(1)}, u32[]{:S(2)}) copy-start(bf16[4,8,128,1,128]{4,2,1,0,3:T(8,128)(2,1)S(1)} %get-tuple-element.309) | copy-start | bytes 3145732
  186.3 49.7 %copy-start.6 = (bf16[64,8,128]{2,0,1:T(8,128)(2,1)S(1)}, bf16[64,8,128]{2,0,1:T(8,128)(2,1)}, u32[]{:S(2)}) copy-start(bf16[64,8,128]{2,0,1:T(8,128)(2,1)} %all_to_all.79) | copy-start | bytes 393220
  286.1 58.7 %copy-start.1 = (bf16[64,8,128]{2,0,1:T(8,128)(2,1)S(1)}, bf16[64,8,128]{2,0,1:T(8,128)(2,1)}, u32[]{:S(2)}) copy-start(bf16[64,8,128]{2,0,1:T(8,128)(2,1)} %all_to_all.77) | copy-start | bytes 393220
  286.1 58.7 %copy-start.4 = (bf16[64,8,128]{2,0,1:T(8,128)(2,1)S(1)}, bf16[64,8,128]{2,0,1:T(8,128)(2,1)}, u32[]{:S(2)}) copy-start(bf16[64,8,128]{2,0,1:T(8,128)(2,1)} %all_to_all.76) | copy-start | bytes 393220
Sparse Core Ops, SparseCore 0:
  18.1 83.1 all-gather.6
  103.9 78.5 all-gather.4
  185.1 78.5 all-gather.8
  266.1 78.6 all-gather.10
where the time goes:
time: 498 us; the launch traced here: 496 us
  waiting for transfers between devices  185 us (37%)
  matrix products  148 us (30%)
  blocking collectives  132 us (27%)
  between operations  14 us (3%)
  local copies, waits for them, and re-layouts  11.9 us (2%)
    all_gather x1, waiting for transfers between devices, on_device(): lax.all_gather(v_rows, 'seq', axis=0, tiled=True)  78.2 us
    all_gather x1, waiting for transfers between devices, on_device(): g_piece = lax.all_gather(g_rows, 'seq', axis=0, tiled=True)  55.2 us
    all_gather x1, waiting for transfers between devices, on_device(): lax.all_gather(k_rows, 'seq', axis=0, tiled=True)  51.3 us
    dot_general x32, matrix products, tile(): jnp.einsum('qhk,qhd->khd', tile_ds, q_tile, preferred_element_type=jnp.fl...  47.7 us
    all_gather x1, blocking collectives, on_device(): lax.all_gather(log_total, 'seq', axis=0, tiled=True)  47.6 us
    all_gather x1, blocking collectives, on_device(): lax.all_gather(grad_dot, 'seq', axis=0, tiled=True)  47.4 us
    dot_general x32, matrix products, tile(): jnp.einsum('qhd,khd->qhk', q_tile, k_heads, preferred_element_type=jnp.fl...  43.6 us
    dot_general x32, matrix products, tile(): jnp.einsum('qhk,qhd->khd', tile_probs.astype(jnp.bfloat16), g_tile, prefe...  37.8 us
  transfers between devices with their start and end apart: 4, of which 3 were waited for; matrix products, arithmetic and copies ran while one was open for 4% of the time, Pallas kernels for 0%

commit v1 on v0

v1 whole, which is shorter than its diff:
```python
import functools
import heapq
import math

import jax
import jax.numpy as jnp
from jax import lax
from jax.experimental import pallas as pl
from jax.experimental.pallas import tpu as pltpu
from jax.sharding import PartitionSpec as P

MESH = pl.DeviceIdType.MESH
BLK = 128
HD = 128
NX = 4
NZ = 8
NH = 8
ROWS = 512
CHUNK = 64
SPLIT = 208
BF16 = jnp.bfloat16
F32 = jnp.float32
NEG = -1e30


def row_range(part):
    half_a, half_b = SPLIT // 32 * 16, SPLIT + (ROWS - SPLIT) // 32 * 16
    return {
        "A": (0, SPLIT),
        "A0": (0, half_a),
        "A1": (half_a, SPLIT),
        "B": (SPLIT, ROWS),
        "B0": (SPLIT, half_b),
        "B1": (half_b, ROWS),
    }[part]


def ring_sends(axis, sources, size, out, kind, prio):
    far = size // 2
    arrived = []
    for (offset, part, dep) in sources:
        if len(part) == 1:
            arrived.append((offset, part, dep))
            halves = [(part, +1, far - 1), (part, -1, far - 1)]
        else:
            arrived.append((offset, part, dep))
            sign = +1 if part[1] == "0" else -1
            halves = [(part, +1, far - 1), (part, -1, far - 1)]
        for (piece, sign, hops) in halves:
            last = dep
            at = offset
            for hop in range(1, hops + 1):
                out.append(dict(kind=kind, axis=axis, sign=sign, origin=at, part=piece, dep=last, left=far - hop, prio=prio))
                last = len(out) - 1
                at = step_offset(at, axis, sign)
                arrived.append((at, piece, last))
            for digit, way in (("0", +1), ("1", -1)):
                if way != sign:
                    continue
                tail = piece if len(piece) == 2 else piece + digit
                if tail[1] != digit:
                    continue
                out.append(dict(kind=kind, axis=axis, sign=sign, origin=at, part=tail, dep=last, left=0, prio=prio))
                arrived.append((step_offset(at, axis, sign), tail, len(out) - 1))
    return arrived


def step_offset(offset, axis, sign):
    ox, oz = offset
    return (ox + sign, oz) if axis == "x" else (ox, oz + sign)


def plan_sends():
    out = []
    for kind in (0, 1):
        own = -1 - kind
        first_a = ring_sends("x", [((0, 0), "A", own)], NX, out, kind, kind * 10)
        first_b = ring_sends("z", [((0, 0), "B", own)], NZ, out, kind, kind * 10)
        ring_sends("z", first_a, NZ, out, kind, kind * 10 + 1)
        ring_sends("x", first_b, NX, out, kind, kind * 10 + 1)
    rate = 46.0e3 * 1.0
    latency = 1.7
    ready_own = {-1: 4.0, -2: 8.0}
    arrival = {}
    free = {}
    start = {}
    waiting = {}
    events = []
    for i, m in enumerate(out):
        if m["dep"] < 0:
            heapq.heappush(events, (ready_own[m["dep"]], i))
    children = {}
    for i, m in enumerate(out):
        if m["dep"] >= 0:
            children.setdefault(m["dep"], []).append(i)
    queues = {("x", 1): [], ("x", -1): [], ("z", 1): [], ("z", -1): []}
    free = {k: 0.0 for k in queues}
    order = []
    while events or any(queues.values()):
        options = []
        for k, q in queues.items():
            if q:
                options.append((max(free[k], q[0][2]), k))
        next_link = min(options) if options else None
        if events and (next_link is None or events[0][0] <= next_link[0]):
            t, i = heapq.heappop(events)
            m = out[i]
            q = queues[(m["axis"], m["sign"])]
            q.append((m["prio"] // 10, -m["left"], t, i))
            q.sort(key=lambda e: (e[0], e[1], e[2], e[3]))
            continue
        t, k = next_link
        _, _, ready, i = queues[k].pop(0)
        m = out[i]
        lo, hi = row_range(m["part"])
        begin = max(free[k], ready)
        free[k] = begin + (hi - lo) * HD * 2 * 2 / rate
        start[i] = begin
        order.append((begin, ready, i))
        for c in children.get(i, []):
            heapq.heappush(events, (free[k] + latency, c))
    order.sort()
    return out, [i for (_, _, i) in order], max(free.values())


SENDS, ORDER, SPAN = plan_sends()


def exchange_kernel(q_ref, k_ref, v_ref, g_ref, kv_ref, qg_ref, send_sem, recv_sem, head_send, head_recv, own_sem):
    seq = lax.axis_index("seq")
    head = lax.axis_index("head")
    x, z = lax.rem(seq, NX), seq // NX

    def chip(cx, cz):
        return lax.rem(cz + 2 * NZ, NZ) * NX + lax.rem(cx + 2 * NX, NX)

    barrier = pltpu.get_barrier_semaphore()
    for shift in range(1, NH):
        pl.semaphore_signal(barrier, inc=1, device_id={"seq": seq, "head": lax.rem(head + shift, NH)}, device_id_type=MESH)
    for (cx, cz) in ((x + 1, z), (x - 1, z), (x, z + 1), (x, z - 1)):
        pl.semaphore_signal(barrier, inc=1, device_id={"seq": chip(cx, cz), "head": head}, device_id_type=MESH)
    pl.semaphore_wait(barrier, NH - 1 + 4)

    targets = ((k_ref, kv_ref, 0), (v_ref, kv_ref, 1), (q_ref, qg_ref, 0), (g_ref, qg_ref, 1))

    def rows_of(dst, which, h):
        return dst.at[seq, which, pl.ds(pl.multiple_of(h * CHUNK, CHUNK), CHUNK), :]

    def columns_of(src, h):
        return src.at[:, pl.ds(pl.multiple_of(h * HD, HD), HD)]

    head_copies = []
    own_copies = []
    for array, (src, dst, which) in enumerate(targets):
        for shift in range(1, NH):
            peer = lax.rem(head + shift, NH)
            copy = pltpu.make_async_remote_copy(
                src_ref=columns_of(src, peer),
                dst_ref=rows_of(dst, which, head),
                send_sem=head_send.at[array, shift],
                recv_sem=head_recv.at[array, shift],
                device_id={"seq": seq, "head": peer},
                device_id_type=MESH,
            )
            copy.start()
            head_copies.append(copy)
        own = pltpu.make_async_copy(columns_of(src, head), rows_of(dst, which, head), own_sem.at[array])
        own.start()
        own_copies.append(own)

    def wait_head(array):
        src, dst, which = targets[array]
        for shift in range(1, NH):
            peer = lax.rem(head + NH - shift, NH)
            pltpu.make_async_remote_copy(
                src_ref=columns_of(src, peer),
                dst_ref=rows_of(dst, which, peer),
                send_sem=head_send.at[array, shift],
                recv_sem=head_recv.at[array, shift],
                device_id={"seq": seq, "head": peer},
                device_id_type=MESH,
            ).wait_recv()
        own_copies[array].wait()

    buffers = (kv_ref, qg_ref)

    def piece(m, ox, oz):
        lo, hi = row_range(m["part"])
        return buffers[m["kind"]].at[chip(x - ox, z - oz), :, lo:hi, :]

    def send(i):
        m = SENDS[i]
        ox, oz = m["origin"]
        target = chip(x + m["sign"], z) if m["axis"] == "x" else chip(x, z + m["sign"])
        return pltpu.make_async_remote_copy(
            src_ref=piece(m, ox, oz),
            dst_ref=piece(m, ox, oz),
            send_sem=send_sem.at[i],
            recv_sem=recv_sem.at[i],
            device_id={"seq": target, "head": head},
            device_id_type=MESH,
        )

    def wait_recv(i):
        m = SENDS[i]
        ox, oz = step_offset(m["origin"], m["axis"], m["sign"])
        source = chip(x - m["sign"], z) if m["axis"] == "x" else chip(x, z - m["sign"])
        pltpu.make_async_remote_copy(
            src_ref=piece(m, ox, oz),
            dst_ref=piece(m, ox, oz),
            send_sem=send_sem.at[i],
            recv_sem=recv_sem.at[i],
            device_id={"seq": source, "head": head},
            device_id_type=MESH,
        ).wait_recv()

    ready = set()
    started = []
    for i in ORDER:
        dep = SENDS[i]["dep"]
        if dep not in ready:
            ready.add(dep)
            if dep < 0:
                wait_head(2 * (-1 - dep))
                wait_head(2 * (-1 - dep) + 1)
            else:
                wait_recv(dep)
        copy = send(i)
        copy.start()
        started.append(copy)
    for i in ORDER:
        if i not in ready:
            wait_recv(i)
    for copy in started:
        copy.wait_send()
    for copy in head_copies:
        copy.wait_send()


def exchange(queries, keys, values, out_grad):
    shape = jax.ShapeDtypeStruct((NX * NZ, 2, ROWS, HD), BF16)
    count = len(SENDS)
    return pl.pallas_call(
        exchange_kernel,
        out_shape=(shape, shape),
        in_specs=[pl.BlockSpec(memory_space=pltpu.VMEM)] * 4,
        out_specs=[pl.BlockSpec(memory_space=pl.ANY)] * 2,
        scratch_shapes=[
            pltpu.SemaphoreType.DMA((count,)),
            pltpu.SemaphoreType.DMA((count,)),
            pltpu.SemaphoreType.DMA((4, NH)),
            pltpu.SemaphoreType.DMA((4, NH)),
            pltpu.SemaphoreType.DMA((4,)),
        ],
        compiler_params=pltpu.CompilerParams(collective_id=0, has_side_effects=True),
    )(queries, keys, values, out_grad)


def dot_nt(a, b):
    return lax.dot_general(a, b, (((1,), (1,)), ((), ())), preferred_element_type=F32)


def dot_nn(a, b):
    return lax.dot_general(a, b, (((1,), (0,)), ((), ())), preferred_element_type=F32)


def dot_tn(a, b):
    return lax.dot_general(a, b, (((0,), (0,)), ((), ())), preferred_element_type=F32)


def attend_kernel(first_ref, touch_ref, blocks_ref, counts_ref, kv_ref, qg_ref, att_ref, dq_ref, dk_ref, dv_ref, s_ref, acc_ref, dk_acc, dv_acc):
    scale = 1.0 / math.sqrt(HD)
    dk_acc[...] = jnp.zeros_like(dk_acc)
    dv_acc[...] = jnp.zeros_like(dv_acc)
    first = first_ref[0]

    def load(ref, which, block):
        return ref[block // 4, which, pl.ds(pl.multiple_of(lax.rem(block, 4) * BLK, BLK), BLK), :]

    def query_block(a, local):
        count = counts_ref[a]
        q = load(qg_ref, 0, a)
        g = load(qg_ref, 1, a)

        def score(t, row_max):
            s = dot_nt(q, load(kv_ref, 0, blocks_ref[a, t])) * scale
            s_ref[t] = s
            return jnp.maximum(row_max, jnp.max(s, axis=1, keepdims=True))

        row_max = lax.fori_loop(0, count, score, jnp.full((BLK, 1), NEG, F32))
        acc_ref[...] = jnp.zeros_like(acc_ref)

        def mix(t, row_sum):
            w = jnp.exp(s_ref[t] - row_max)
            acc_ref[...] += dot_nn(w.astype(BF16), load(kv_ref, 1, blocks_ref[a, t]))
            return row_sum + jnp.sum(w, axis=1, keepdims=True)

        row_sum = lax.fori_loop(0, count, mix, jnp.zeros((BLK, 1), F32))
        att = (acc_ref[...] / row_sum).astype(BF16)
        total = row_max + jnp.log(row_sum)
        grad_dot = jnp.sum(g.astype(F32) * att.astype(F32), axis=1, keepdims=True)

        def pair(t):
            block = blocks_ref[a, t]
            p = jnp.exp(s_ref[t] - total)
            dp = dot_nt(g, load(kv_ref, 1, block))
            return block, p, (p * (dp - grad_dot)).astype(BF16)

        def add_key(slot, p, ds):
            dk_acc[slot] += dot_tn(ds, q)
            dv_acc[slot] += dot_tn(p.astype(BF16), g)

        if local:
            acc_ref[...] = jnp.zeros_like(acc_ref)

            def back(t, carry):
                block, p, ds = pair(t)
                acc_ref[...] += dot_nn(ds, load(kv_ref, 0, block))
                slot = block - first

                @pl.when((slot >= 0) & (slot < 4))
                def _():
                    add_key(slot, p, ds)

                return carry

            lax.fori_loop(0, count, back, 0)
            rows = pl.ds(pl.multiple_of((a - first) * BLK, BLK), BLK)
            att_ref[rows, :] = att
            dq_ref[rows, :] = (acc_ref[...] * scale).astype(BF16)
        else:

            def back(t, carry):
                slot = blocks_ref[a, t] - first

                @pl.when((slot >= 0) & (slot < 4))
                def _():
                    _, p, ds = pair(t)
                    add_key(slot, p, ds)

                return carry

            lax.fori_loop(0, count, back, 0)

    def own(i, carry):
        query_block(first + i, True)
        return carry

    lax.fori_loop(0, 4, own, 0)

    def other(a, carry):
        @pl.when(touch_ref[a] > 0)
        def _():
            query_block(a, False)

        return carry

    lax.fori_loop(0, 128, other, 0)
    for slot in range(4):
        dk_ref[slot * BLK : (slot + 1) * BLK, :] = (dk_acc[slot] * scale).astype(BF16)
        dv_ref[slot * BLK : (slot + 1) * BLK, :] = dv_acc[slot].astype(BF16)


def attend(first, touch, key_blocks, counts, kv, qg):
    shape = jax.ShapeDtypeStruct((ROWS, HD), BF16)
    smem = pl.BlockSpec(memory_space=pltpu.SMEM)
    vmem = pl.BlockSpec(memory_space=pltpu.VMEM)
    return pl.pallas_call(
        attend_kernel,
        out_shape=(shape,) * 4,
        in_specs=[smem] * 4 + [vmem] * 2,
        out_specs=[vmem] * 4,
        scratch_shapes=[
            pltpu.VMEM((8, BLK, BLK), F32),
            pltpu.VMEM((BLK, HD), F32),
            pltpu.VMEM((4, BLK, HD), F32),
            pltpu.VMEM((4, BLK, HD), F32),
        ],
    )(first, touch, key_blocks, counts, kv, qg)


def on_device(queries, keys, values, out_grad, key_blocks, counts):
    seq = lax.axis_index("seq")
    kv, qg = exchange(queries, keys, values, out_grad)
    used = jnp.arange(key_blocks.shape[1])[None, :] < counts[:, None]
    touch = jnp.any(used & (key_blocks // 4 == seq), axis=1)
    touch = (touch & (jnp.arange(key_blocks.shape[0]) // 4 != seq)).astype(jnp.int32)
    first = (seq * 4).reshape(1).astype(jnp.int32)
    return attend(first, touch, key_blocks, counts, kv, qg)


def solution(mesh):
    rows = P(("seq", "head"), None)
    out = P("seq", "head")
    return jax.shard_map(
        on_device,
        mesh=mesh,
        in_specs=(rows,) * 4 + (P(), P()),
        out_specs=(out,) * 4,
        check_vma=False,
    )
```

time: 498 us -> 165 us (0.33)
  the two profiles are of different devices: /device:TPU:8 before, /device:TPU:198 now
where the time goes in v1:
time: 165 us; the launch traced here: 163 us
  Pallas kernels  160 us (97%)
    pallas_call x1, Pallas kernels, exchange(): pl.pallas_call(exchange_kernel, out_shape=(shape, shape), in_specs=[pl.Bl...  110 us
    pallas_call x1, Pallas kernels, attend(): pl.pallas_call(attend_kernel, out_shape=(shape,) * 4, in_specs=[smem] * 4...  50.4 us

profile of v1, /device:TPU:198, one launch (start us, length us, event | category | flops | bytes accessed | tf_op | source)
XLA Modules:
  0.0 163.4 jit_solution(148331296853348230)
XLA Ops:
  0.6 0.7 fusion.3
  1.4 0.5 and_convert_fusion.touch_ref
  1.9 1.4 copy.10.blocks_ref
  3.3 109.8 %shard_map.93 = (bf16[32,2,512,128]{3,2,1,0:T(8,128)(2,1)}, bf16[32,2,512,128]{3,2,1,0:T(8,128)(2,1)}) custom-call(bf16[64,1024]{1,0:T(8,128)(2,1)} %q_ref.1, bf16[64,1024]{1,0:T(8,128)(2,1)} %k_ref.1, bf16[64,1024]{1,0:T(8,128)(2,1)} %v_ref.1, bf16[64,1024]{1,0:T(8,128)(2,1)} %g_ref.1), custom_call_target="tpu_custom_call" | custom-call | tf_op jit(solution)/shard_map/pallas_call | solution.py:243
  113.1 50.4 %shard_map.94 = (bf16[512,128]{1,0:T(8,128)(2,1)}, bf16[512,128]{1,0:T(8,128)(2,1)}, bf16[512,128]{1,0:T(8,128)(2,1)}, bf16[512,128]{1,0:T(8,128)(2,1)}) custom-call(s32[1]{0:T(128)} %bitcast.first_ref, s32[128]{0:T(128)} %and_convert_fusion.touch_ref, s32[128,8]{1,0:T(8,128)} %copy.10.blocks_ref, s32[128]{0:T(128)} %counts_ref.1, ...), custom_call_target="tpu_custom_call" | custom-call | tf_op jit(solution)/shard_map/pallas_call | solution.py:368

commit v2 on v1

--- a/solution.py
+++ b/solution.py
@@ -379,14 +379,455 @@
     )(first, touch, key_blocks, counts, kv, qg)
 
 
+SLOTS = 26
+LAG = 2
+LATE = 6
+CTL = 1024
+AT_CODE = 64
+AT_LAST = 96
+AT_COUNT = 97
+AT_USED = 100
+AT_LIST = 128
+
+
+def plan_kernel(mine_ref, used_ref, blocks_ref, counts_ref, ctl_ref, words_ref, words, where_kv, where_qg, sem):
+    seq = lax.axis_index("seq")
+    x, z = lax.rem(seq, NX), seq // NX
+    lane = lax.broadcasted_iota(jnp.int32, (BLK, BLK), 1)
+    count = counts_ref[...]
+    hits = jnp.zeros((BLK, BLK), F32)
+    for t in range(8):
+        live = (blocks_ref[:, t : t + 1] == lane) & (count > t)
+        hits = jnp.where(live, 1.0, hits)
+    row = lax.broadcasted_iota(jnp.int32, (32, BLK), 0)
+    col = lax.broadcasted_iota(jnp.int32, (32, BLK), 1)
+    device = lax.rem(row, NZ) * NX + row // NZ
+    group = jnp.where(col // 4 == device, 1.0, 0.0)
+    need_kv = dot_nn(group, hits)
+    need_qg = dot_nt(group, hits)
+    jrow = lax.broadcasted_iota(jnp.int32, (8, BLK), 0)
+    jcol = lax.broadcasted_iota(jnp.int32, (8, BLK), 1)
+    mine = jcol - seq * 4
+    power = jnp.where(mine == 0, 1.0, jnp.where(mine == 1, 2.0, jnp.where(mine == 2, 4.0, jnp.where(mine == 3, 8.0, 0.0))))
+    bits = dot_nt(power, hits)
+
+    origin = jcol // 16
+    delta = lax.rem(jrow - origin + NZ, NZ)
+    even = lax.rem(jcol, 2) == 0
+    ahead = (delta >= 1) & ((delta < 4) | ((delta == 4) & even))
+    behind = (delta > 4) | ((delta == 4) & jnp.logical_not(even))
+    far = delta.astype(F32)
+    ident = (127 - jcol).astype(F32)
+    here = origin == jrow
+
+    chains = []
+    for sign in (1, -1):
+        for column in range(NX):
+            keys = []
+            for need, base in ((need_kv, 128.0), (need_qg, 0.0)):
+                part = need[column * NZ : (column + 1) * NZ, :] > 0.5
+                hop = jnp.where(part & ahead, far, 0.0) if sign == 1 else jnp.where(part & behind, 8.0 - far, 0.0)
+                most = jnp.max(hop, axis=0, keepdims=True)
+                keys.append(jnp.where(here & (most > 0.5), most * 256.0 + base + ident, 0.0))
+            chains.append(dict(sign=sign, keys=keys, sent=[], out=jnp.zeros((8, BLK), F32)))
+    zero = jnp.zeros((8, BLK), F32)
+    last = zero
+    for t in range(SLOTS):
+        for c in chains:
+            if t >= LAG:
+                before = c["sent"][t - LAG]
+                passing = pltpu.roll(before, 1 if c["sign"] == 1 else 7, 0) - 256.0
+                through = passing > 255.5
+            best = c["keys"][0] if t < LATE else jnp.maximum(c["keys"][0], c["keys"][1])
+            best = jnp.broadcast_to(jnp.max(best, axis=1, keepdims=True), (8, BLK))
+            if t >= LAG:
+                taken = jnp.where(through, -1.0, best)
+                sent = jnp.where(through, passing, best)
+                mark = jnp.where(through, -passing, best)
+            else:
+                taken, sent, mark = best, best, best
+            c["keys"] = [jnp.where(k == taken, 0.0, k) for k in c["keys"]]
+            c["sent"].append(sent)
+            c["out"] = jnp.where(jcol == t, mark, c["out"])
+    unfit = zero
+    for c in chains:
+        unfit = jnp.maximum(unfit, jnp.maximum(c["keys"][0], c["keys"][1]))
+        for t in range(SLOTS - LAG, SLOTS):
+            unfit = jnp.maximum(unfit, c["sent"][t] - 511.0)
+    unfit = jnp.max(jnp.max(unfit, axis=1, keepdims=True), axis=0, keepdims=True)
+    ours = []
+    for half in range(2):
+        pick = zero
+        for column in range(NX):
+            pick = jnp.where(x == column, chains[half * NX + column]["out"], pick)
+        ours.append(pick)
+    words_ref[0:8, :] = ours[0].astype(jnp.int32)
+    words_ref[8:16, :] = ours[1].astype(jnp.int32)
+    words_ref[16:24, :] = bits.astype(jnp.int32)
+    words_ref[24:32, :] = jnp.broadcast_to(unfit, (8, BLK)).astype(jnp.int32)
+    copy = pltpu.make_async_copy(words_ref, words, sem)
+    copy.start()
+    copy.wait()
+
+    ctl_ref[AT_LAST] = words[24, 0]
+    for i in range(4):
+        ctl_ref[AT_USED + i] = used_ref[i]
+
+    def clear(i, carry):
+        where_kv[i] = 0
+        where_qg[i] = 0
+        return carry
+
+    lax.fori_loop(0, BLK, clear, 0)
+    for i in range(16):
+        where_kv[z * 16 + i] = i
+        where_qg[z * 16 + i] = i
+    sources = (lax.rem(z + NZ - 1, NZ), lax.rem(z + 1, NZ))
+    for half in range(2):
+
+        def slot(t, carry):
+            ctl_ref[half * SLOTS + t] = words[half * 8 + z, t]
+            value = jnp.abs(words[half * 8 + sources[half], t])
+            block = 127 - (value & 127)
+            spot = 16 + half * SLOTS + t
+
+            @pl.when((value >= 256) & ((value & 128) > 0))
+            def _():
+                where_kv[block] = spot
+
+            @pl.when((value >= 256) & ((value & 128) == 0))
+            def _():
+                where_qg[block] = spot
+
+            return carry
+
+        lax.fori_loop(0, SLOTS, slot, 0)
+    for i in range(4):
+        for t in range(8):
+            block = jnp.where(t < used_ref[i], mine_ref[i * 8 + t], seq * 4 + i)
+            ctl_ref[AT_CODE + i * 8 + t] = where_kv[block]
+
+    def entry(a, n):
+        mask = words[16, a]
+
+        @pl.when(mask > 0)
+        def _():
+            ctl_ref[AT_LIST + 4 * n] = a
+            ctl_ref[AT_LIST + 4 * n + 1] = where_qg[a]
+            ctl_ref[AT_LIST + 4 * n + 2] = mask
+
+        return n + jnp.where(mask > 0, 1, 0)
+
+    ctl_ref[AT_COUNT] = lax.fori_loop(0, BLK, entry, 0)
+
+
+def make_plan(mine, used, key_blocks, counts):
+    smem = pl.BlockSpec(memory_space=pltpu.SMEM)
+    vmem = pl.BlockSpec(memory_space=pltpu.VMEM)
+    return pl.pallas_call(
+        plan_kernel,
+        out_shape=jax.ShapeDtypeStruct((CTL,), jnp.int32),
+        in_specs=[smem, smem, vmem, vmem],
+        out_specs=smem,
+        scratch_shapes=[
+            pltpu.VMEM((32, BLK), jnp.int32),
+            pltpu.SMEM((32, BLK), jnp.int32),
+            pltpu.SMEM((BLK,), jnp.int32),
+            pltpu.SMEM((BLK,), jnp.int32),
+            pltpu.SemaphoreType.DMA,
+        ],
+    )(mine, used, key_blocks, counts)
+
+
+def pick(cond, a, b):
+    return lax.select(cond, a, b)
+
+
+def route_kernel(
+    ctl_ref, q_ref, k_ref, v_ref, g_ref,
+    att_ref, dq_ref, kv_ref, qg_ref, recv_ref, stats_ref,
+    send_ref, kcat, vcat, mine_stats,
+    head_send, head_recv, own_sem, x_send, x_recv, z_send, z_recv, s_send, s_recv,
+):
+    seq = lax.axis_index("seq")
+    head = lax.axis_index("head")
+    x, z = lax.rem(seq, NX), seq // NX
+
+    def chip(cx, cz):
+        return lax.rem(cz + 2 * NZ, NZ) * NX + lax.rem(cx + 2 * NX, NX)
+
+    barrier = pltpu.get_barrier_semaphore()
+    for shift in range(1, NH):
+        pl.semaphore_signal(barrier, inc=1, device_id={"seq": seq, "head": lax.rem(head + shift, NH)}, device_id_type=MESH)
+    for shift in range(1, NX * NZ):
+        pl.semaphore_signal(barrier, inc=1, device_id={"seq": lax.rem(seq + shift, NX * NZ), "head": head}, device_id_type=MESH)
+    pl.semaphore_wait(barrier, NH - 1 + NX * NZ - 1)
+
+    targets = ((k_ref, kv_ref, 0), (v_ref, kv_ref, 1), (q_ref, qg_ref, 0), (g_ref, qg_ref, 1))
+
+    def rows_of(dst, which, h):
+        start = pl.multiple_of(which * BLK + lax.rem(h, 2) * CHUNK, CHUNK)
+        return dst.at[4 * x + h // 2, pl.ds(start, CHUNK), :]
+
+    def columns_of(src, h):
+        return src.at[:, pl.ds(pl.multiple_of(h * HD, HD), HD)]
+
+    def head_copy(array, peer_from, peer_to, shift):
+        src, dst, which = targets[array]
+        return pltpu.make_async_remote_copy(
+            src_ref=columns_of(src, peer_to),
+            dst_ref=rows_of(dst, which, peer_from),
+            send_sem=head_send.at[array, shift],
+            recv_sem=head_recv.at[array, shift],
+            device_id={"seq": seq, "head": peer_to},
+            device_id_type=MESH,
+        )
+
+    started = []
+    own_copies = []
+    for array, (src, dst, which) in enumerate(targets):
+        for shift in range(1, NH):
+            copy = head_copy(array, head, lax.rem(head + shift, NH), shift)
+            copy.start()
+            started.append(copy)
+        own = pltpu.make_async_copy(columns_of(src, head), rows_of(dst, which, head), own_sem.at[array])
+        own.start()
+        own_copies.append(own)
+
+    def wait_head(array):
+        for shift in range(1, NH):
+            peer = lax.rem(head + NH - shift, NH)
+            head_copy(array, peer, peer, shift).wait_recv()
+        own_copies[array].wait()
+
+    rows = (kv_ref, qg_ref)
+    x_plan = ((1, 0, 0), (-1, 0, 2), (1, 0, 2), (-1, 0, 0), (1, 1, 0), (-1, -1, 2))
+
+    def x_copy(kind, i, arriving):
+        sign, offset, first = x_plan[i]
+        origin = lax.rem(x - offset - (sign if arriving else 0) + 2 * NX, NX)
+        piece = rows[kind].at[pl.ds(4 * origin + first, 2)]
+        other = chip(x - sign, z) if arriving else chip(x + sign, z)
+        return pltpu.make_async_remote_copy(
+            src_ref=piece, dst_ref=piece, send_sem=x_send.at[kind, i], recv_sem=x_recv.at[kind, i],
+            device_id={"seq": other, "head": head}, device_id_type=MESH,
+        )
+
+    def x_start(kind, i):
+        copy = x_copy(kind, i, False)
+        copy.start()
+        started.append(copy)
+
+    def z_copy(half, t, arriving):
+        sign = 1 if half == 0 else -1
+        other = chip(x, z - sign) if arriving else chip(x, z + sign)
+        slot = half * SLOTS + t
+        return pltpu.make_async_remote_copy(
+            src_ref=send_ref.at[slot], dst_ref=recv_ref.at[slot], send_sem=z_send.at[slot], recv_sem=z_recv.at[slot],
+            device_id={"seq": other, "head": head}, device_id_type=MESH,
+        )
+
+    wait_head(0)
+    wait_head(1)
+    for i in range(4):
+        x_start(0, i)
+    wait_head(2)
+    wait_head(3)
+    x_copy(0, 0, True).wait_recv()
+    x_start(0, 4)
+    x_copy(0, 1, True).wait_recv()
+    x_start(0, 5)
+    for i in range(4):
+        x_start(1, i)
+    for i in range(2, 6):
+        x_copy(0, i, True).wait_recv()
+
+    for t in range(SLOTS):
+        if t == 2:
+            x_copy(1, 0, True).wait_recv()
+            x_start(1, 4)
+            x_copy(1, 1, True).wait_recv()
+            x_start(1, 5)
+        if t == LATE:
+            for i in range(2, 6):
+                x_copy(1, i, True).wait_recv()
+        for half in range(2):
+            slot = half * SLOTS + t
+            value = ctl_ref[slot]
+            size = jnp.abs(value)
+            index = (127 - (size & 127)) & 15
+            data = kv_ref[index]
+            if t >= LATE:
+                data = pick((size & 128) > 0, data, qg_ref[index])
+            if t >= LAG:
+                z_copy(half, t - LAG, True).wait_recv()
+                data = pick(value < 0, recv_ref[slot - LAG], data)
+            send_ref[slot] = data
+        for half in range(2):
+            copy = z_copy(half, t, False)
+            copy.start()
+            started.append(copy)
+    for t in range(SLOTS - LAG, SLOTS):
+        for half in range(2):
+            z_copy(half, t, True).wait_recv()
+
+    scale = 1.0 / math.sqrt(HD)
+    key_at = lax.broadcasted_iota(jnp.int32, (BLK, 8 * BLK), 1)
+
+    def query_block(i, carry):
+        for t in range(8):
+            code = ctl_ref[AT_CODE + i * 8 + t]
+            near = kv_ref[jnp.minimum(code, 15)]
+            moved = recv_ref[jnp.maximum(code - 16, 0)]
+            data = pick(code < 16, near, moved)
+            kcat[t * BLK : (t + 1) * BLK, :] = data[0:BLK]
+            vcat[t * BLK : (t + 1) * BLK, :] = data[BLK : 2 * BLK]
+        own = qg_ref[4 * x + i]
+        q, g = own[0:BLK], own[BLK : 2 * BLK]
+        s = dot_nt(q, kcat[...]) * scale
+        s = jnp.where(key_at < ctl_ref[AT_USED + i] * BLK, s, NEG)
+        row_max = jnp.max(s, axis=1, keepdims=True)
+        w = jnp.exp(s - row_max)
+        row_sum = jnp.sum(w, axis=1, keepdims=True)
+        att = (dot_nn(w.astype(BF16), vcat[...]) / row_sum).astype(BF16)
+        total = row_max + jnp.log(row_sum)
+        grad_dot = jnp.sum(g.astype(F32) * att.astype(F32), axis=1, keepdims=True)
+        p = jnp.exp(s - total)
+        ds = (p * (dot_nt(g, vcat[...]) - grad_dot)).astype(BF16)
+        at = pl.ds(pl.multiple_of(i * BLK, BLK), BLK)
+        att_ref[at, :] = att
+        dq_ref[at, :] = (dot_nn(ds, kcat[...]) * scale).astype(BF16)
+        mine_stats[pl.ds(i, 1), :] = jnp.transpose(jnp.broadcast_to(total, (BLK, BLK)))[0:1, :]
+        mine_stats[pl.ds(i + 4, 1), :] = jnp.transpose(jnp.broadcast_to(grad_dot, (BLK, BLK)))[0:1, :]
+        return carry
+
+    lax.fori_loop(0, 4, query_block, 0)
+
+    def stat_copy(shift, origin, target):
+        return pltpu.make_async_remote_copy(
+            src_ref=mine_stats, dst_ref=stats_ref.at[origin], send_sem=s_send.at[shift], recv_sem=s_recv.at[shift],
+            device_id={"seq": target, "head": head}, device_id_type=MESH,
+        )
+
+    for shift in range(1, NX * NZ):
+        copy = stat_copy(shift, seq, lax.rem(seq + shift, NX * NZ))
+        copy.start()
+        started.append(copy)
+    own = pltpu.make_async_copy(mine_stats, stats_ref.at[seq], s_recv.at[0])
+    own.start()
+    for shift in range(1, NX * NZ):
+        peer = lax.rem(seq + NX * NZ - shift, NX * NZ)
+        stat_copy(shift, peer, peer).wait_recv()
+    own.wait()
+    for copy in started:
+        copy.wait_send()
+
+
+def route(ctl, queries, keys, values, out_grad):
+    smem = pl.BlockSpec(memory_space=pltpu.SMEM)
+    vmem = pl.BlockSpec(memory_space=pltpu.VMEM)
+    out = jax.ShapeDtypeStruct((ROWS, HD), BF16)
+    near = jax.ShapeDtypeStruct((16, 2 * BLK, HD), BF16)
+    moved = jax.ShapeDtypeStruct((2 * SLOTS, 2 * BLK, HD), BF16)
+    stats = jax.ShapeDtypeStruct((NX * NZ, 8, BLK), F32)
+    dma = pltpu.SemaphoreType.DMA
+    return pl.pallas_call(
+        route_kernel,
+        out_shape=(out, out, near, near, moved, stats),
+        in_specs=[smem] + [vmem] * 4,
+        out_specs=[vmem] * 6,
+        scratch_shapes=[
+            pltpu.VMEM((2 * SLOTS, 2 * BLK, HD), BF16),
+            pltpu.VMEM((8 * BLK, HD), BF16),
+            pltpu.VMEM((8 * BLK, HD), BF16),
+            pltpu.VMEM((8, BLK), F32),
+            dma((4, NH)), dma((4, NH)), dma((4,)),
+            dma((2, 6)), dma((2, 6)),
+            dma((2 * SLOTS,)), dma((2 * SLOTS,)),
+            dma((NX * NZ,)), dma((NX * NZ,)),
+        ],
+        compiler_params=pltpu.CompilerParams(collective_id=1, has_side_effects=True),
+    )(ctl, queries, keys, values, out_grad)
+
+
+def keys_kernel(ctl_ref, kv_ref, qg_ref, recv_ref, stats_ref, dk_ref, dv_ref, now, dk_acc, dv_acc):
+    scale = 1.0 / math.sqrt(HD)
+    x = lax.rem(lax.axis_index("seq"), NX)
+    dk_acc[...] = jnp.zeros_like(dk_acc)
+    dv_acc[...] = jnp.zeros_like(dv_acc)
+
+    def entry(n, carry):
+        a = ctl_ref[AT_LIST + 4 * n]
+        code = ctl_ref[AT_LIST + 4 * n + 1]
+        mask = ctl_ref[AT_LIST + 4 * n + 2]
+
+        @pl.when(code < 16)
+        def _():
+            now[...] = qg_ref[code]
+
+        @pl.when(code >= 16)
+        def _():
+            now[...] = recv_ref[code - 16]
+
+        q, g = now[0:BLK, :], now[BLK : 2 * BLK, :]
+        total = stats_ref[a // 4, pl.ds(lax.rem(a, 4), 1), :]
+        grad_dot = stats_ref[a // 4, pl.ds(lax.rem(a, 4) + 4, 1), :]
+        for j in range(4):
+
+            @pl.when((mask & (1 << j)) > 0)
+            def _():
+                k = kv_ref[4 * x + j, 0:BLK, :]
+                v = kv_ref[4 * x + j, BLK : 2 * BLK, :]
+                p = jnp.exp(dot_nt(k, q) * scale - total)
+                ds = (p * (dot_nt(v, g) - grad_dot)).astype(BF16)
+                dk_acc[j] += dot_nn(ds, q)
+                dv_acc[j] += dot_nn(p.astype(BF16), g)
+
+        return carry
+
+    lax.fori_loop(0, ctl_ref[AT_COUNT], entry, 0)
+    for j in range(4):
+        dk_ref[j * BLK : (j + 1) * BLK, :] = (dk_acc[j] * scale).astype(BF16)
+        dv_ref[j * BLK : (j + 1) * BLK, :] = dv_acc[j].astype(BF16)
+
+
+def key_grads(ctl, kv, qg, recv, stats):
+    smem = pl.BlockSpec(memory_space=pltpu.SMEM)
+    vmem = pl.BlockSpec(memory_space=pltpu.VMEM)
+    out = jax.ShapeDtypeStruct((ROWS, HD), BF16)
+    return pl.pallas_call(
+        keys_kernel,
+        out_shape=(out, out),
+        in_specs=[smem] + [vmem] * 4,
+        out_specs=[vmem] * 2,
+        scratch_shapes=[
+            pltpu.VMEM((2 * BLK, HD), BF16),
+            pltpu.VMEM((4, BLK, HD), F32),
+            pltpu.VMEM((4, BLK, HD), F32),
+        ],
+    )(ctl, kv, qg, recv, stats)
+
+
 def on_device(queries, keys, values, out_grad, key_blocks, counts):
     seq = lax.axis_index("seq")
-    kv, qg = exchange(queries, keys, values, out_grad)
-    used = jnp.arange(key_blocks.shape[1])[None, :] < counts[:, None]
-    touch = jnp.any(used & (key_blocks // 4 == seq), axis=1)
-    touch = (touch & (jnp.arange(key_blocks.shape[0]) // 4 != seq)).astype(jnp.int32)
-    first = (seq * 4).reshape(1).astype(jnp.int32)
-    return attend(first, touch, key_blocks, counts, kv, qg)
+    mine = lax.dynamic_slice_in_dim(key_blocks, 4 * seq, 4, 0).reshape(32)
+    used = lax.dynamic_slice_in_dim(counts, 4 * seq, 4, 0)
+    ctl = make_plan(mine, used, key_blocks, counts[:, None])
+
+    def sparse(_):
+        att, dq, kv, qg, recv, stats = route(ctl, queries, keys, values, out_grad)
+        dk, dv = key_grads(ctl, kv, qg, recv, stats)
+        return att, dq, dk, dv
+
+    def dense(_):
+        kv, qg = exchange(queries, keys, values, out_grad)
+        live = jnp.arange(key_blocks.shape[1])[None, :] < counts[:, None]
+        touch = jnp.any(live & (key_blocks // 4 == seq), axis=1)
+        touch = (touch & (jnp.arange(key_blocks.shape[0]) // 4 != seq)).astype(jnp.int32)
+        first = (seq * 4).reshape(1).astype(jnp.int32)
+        return tuple(attend(first, touch, key_blocks, counts, kv, qg))
+
+    return lax.cond(ctl[AT_LAST] <= 0, sparse, dense, 0)
 
 
 def solution(mesh):

time: 165 us -> 125 us (0.76)
  the two profiles are of different devices: /device:TPU:198 before, /device:TPU:8 now
where the time goes in v2:
time: 125 us; the launch traced here: 124 us
  Pallas kernels  115 us (92%)
  local copies, waits for them, and re-layouts  7.37 us (6%)
  between operations  1.3 us (1%)
    pallas_call x1, Pallas kernels, route(): pl.pallas_call(route_kernel, out_shape=(out, out, near, near, moved, stat...  99.2 us
    pallas_call x1, Pallas kernels, make_plan(): pl.pallas_call(plan_kernel, out_shape=jax.ShapeDtypeStruct((CTL,), jnp.in...  8.4 us
    pallas_call x1, Pallas kernels, key_grads(): pl.pallas_call(keys_kernel, out_shape=(out, out), in_specs=[smem] + [vmem...  7.43 us
    unnamed x3, local copies, waits for them, and re-layouts  2.72 us

profile of v2, /device:TPU:8, one launch (start us, length us, event | category | flops | bytes accessed | tf_op | source)
XLA Modules:
  0.0 123.7 jit_solution(13334162152423384628)
XLA Ops:
  0.6 1.2 %dynamic_slice.7.used_ref = s32[4]{0:T(128)} dynamic-slice(s32[128]{0:T(128)} %param.13, s32[]{:T(128)S(6)} %select_n.14), dynamic_slice_sizes={4} | dynamic-slice | bytes 36 | tf_op jit(solution)/shard_map/dynamic_slice | solution.py:814
  1.9 0.8 constant_dynamic-slice_fusion
  2.6 0.1 copy.18
  2.7 0.6 reshape.19.mine_ref
  3.3 1.4 %copy.20.counts_ref = s32[128,1]{1,0:T(8,128)} copy(s32[128,1]{0,1:T(1,128)} %bitcast.3) | data formatting | bytes 1024 | tf_op jit(solution)/shard_map/broadcast_in_dim | solution.py:815
  4.7 1.4 %copy.19.blocks_ref = s32[128,8]{1,0:T(8,128)} copy(s32[128,8]{0,1:T(8,128)} %param.12) | data formatting | bytes 8192 | tf_op args[4]
  6.1 8.4 %shard_map.101 = s32[1024]{0:T(1024)S(1)} custom-call(s32[32]{0:T(128)} %reshape.19.mine_ref, s32[4]{0:T(128)} %dynamic_slice.7.used_ref, s32[128,8]{1,0:T(8,128)} %copy.19.blocks_ref, s32[128,1]{1,0:T(8,128)} %copy.20.counts_ref), custom_call_target="tpu_custom_call" | custom-call | tf_op jit(solution)/shard_map/pallas_call | solution.py:527
  14.5 0.6 slice.3
  15.8 106.7 %conditional.1 = ((bf16[512,128]{1,0:T(8,128)(2,1)S(1)}, bf16[512,128]{1,0:T(8,128)(2,1)S(1)}, bf16[512,128]{1,0:T(8,128)(2,1)}, bf16[512,128]{1,0:T(8,128)(2,1)})) conditional(s32[]{:T(128)} %bitcast.2, (s32[]{:T(128)}, s32[128]{0:T(128)}, s32[128,8]{0,1:T(8,128)}, bf16[64,1024]{1,0:T(8,128)(2,1)}, bf16[64,1024]{1,0:T(8,128)(2,1)}, ...), branch_computations={%region_0.2_spmd, %region_2.3_spmd} | conditional | flops 20737 | bytes 30008 | solution.py:830
  15.8 99.2 %branch_1_fun.2 = (bf16[512,128]{1,0:T(8,128)(2,1)S(1)}, bf16[512,128]{1,0:T(8,128)(2,1)S(1)}, bf16[16,256,128]{2,1,0:T(8,128)(2,1)}, bf16[16,256,128]{2,1,0:T(8...) custom-call(s32[1024]{0:T(1024)S(1)} %get-tuple-element.33.ctl_ref, ...), custom_call_target="tpu_custom_call" | custom-call | tf_op jit(solution)/shard_map/cond/branch_1_fun/pallas_call | solution.py:734
  115.0 7.4 %branch_1_fun.3 = (bf16[512,128]{1,0:T(8,128)(2,1)}, bf16[512,128]{1,0:T(8,128)(2,1)}) custom-call(s32[1024]{0:T(1024)S(1)} %get-tuple-element.33.ctl_ref, bf16[16,256,128]{2,1,0:T(8,128)(2,1)} %get-tuple-element.40.kv_ref, bf16[16,256,128]{2,1,0:T(8,128)(2,1)} %get-tuple-element.41.qg_ref, bf16[52,256,128]{2,1,0:T(8,128)(2,1)} %get-tuple-element.42.recv_ref, ...), custom_call_target="tpu_custom_call" | custom-call | tf_op jit(solution)/shard_map/cond/branch_1_fun/pallas_call | solution.py:798
  122.4 0.7 copy.32
  123.1 0.7 copy.33
